TPU v7x, 256 devices: a whole 4x4x8 slice. The times are simulated.
256 devices in a mesh: energy: 128 (over y_lo, x, z, core), mode: 2 (over y_hi).
Axes of the slice: x: 4, y: 4 (y_hi: 2, y_lo: 2; y = y_hi * 2 + y_lo), z: 8, core: 2. Of those that a mesh axis runs over, the one named last changes fastest.
Arguments:
- spectral: float32 [128, 896, 896], P('energy', 'mode'), may hold values from -6 to 6
- coupling: bfloat16 [2, 896, 896], P('mode'), may hold values from -0.1875 to 0.1875
- offsets: int32 [2], P('mode'), may hold values from 1 to 2, as said below
- occupation: int32 [2, 128], P('mode', 'energy'), may hold values from 0 to 3
Outputs:
- self_energy: float32 [128, 896, 896], P('energy', 'mode')
Inputs may be any that keep to these rules, and one draw needn't show every extreme that they name: `offsets`: each offset from 1 to 2 belongs to exactly 1 modes.
All inputs are finite; a program needn't handle non-finite values.
Results may differ from a plain program's by a relative error of at most 0.0041.
Values sent between devices are 32-bit elements; how exact they have to be, the bound alone decides.
A program may use at most 64 MiB of HBM per device.

v0:
```python
import jax
import jax.numpy as jnp
from jax import lax
from jax.sharding import PartitionSpec as P

KMAX = 2


def passed_along(value, axis, steps):
    count = lax.axis_size(axis)
    first, last = (max(0, -steps), min(count, count - steps))
    return lax.ppermute(value, axis, [(source, source + steps) for source in range(first, last)])


def split_up(value, dim, devices):
    shape = value.shape
    parts = value.reshape(*shape[:dim], devices, shape[dim] // devices, *shape[dim + 1 :])
    return jnp.moveaxis(parts, dim, 0)


def summed_on_arrival(value, axis, dim):
    parts = split_up(value, dim, lax.axis_size(axis))
    arrived = lax.all_to_all(parts, axis, split_axis=0, concat_axis=0, tiled=True)
    return arrived.sum(axis=0)


def collect_rim(own_block, max_offset):
    per_device = own_block.shape[0]
    farthest = -(-max_offset // per_device)
    requests = []
    for distance in range(farthest, 0, -1):
        requests.append((distance, max(0, distance * per_device - max_offset), per_device))
    for distance in range(1, farthest + 1):
        requests.append((-distance, 0, min(per_device, max_offset - (distance - 1) * per_device)))
    lower_parts = []
    upper_parts = []
    for shift_by, first_row, last_row in requests:
        arrived = passed_along(own_block, "energy", shift_by)
        if shift_by > 0:
            lower_parts.append(arrived)
        else:
            upper_parts.append(arrived)
    return jnp.concatenate(lower_parts + [own_block] + upper_parts, axis=0)


def shards(spectral, coupling, offsets, occupation):
    max_offset = KMAX
    full_block = lax.all_gather(spectral, "mode", axis=1, tiled=True)
    window = collect_rim(full_block, max_offset)
    per_device = spectral.shape[0]
    window_len = window.shape[0]
    position = lax.broadcasted_iota(jnp.int32, (1, per_device, window_len), 2)
    energy_pos = lax.broadcasted_iota(jnp.int32, (1, per_device, window_len), 1) + max_offset
    offset_col = offsets[:, None, None]
    emission = (occupation + 1).astype(jnp.float32)[:, :, None]
    absorption = occupation.astype(jnp.float32)[:, :, None]
    weights_table = jnp.where(position == energy_pos - offset_col, emission, 0.0)
    weights_table = weights_table + jnp.where(position == energy_pos + offset_col, absorption, 0.0)
    combined = jnp.einsum(
        "mew,wij->meij", weights_table, window, precision=lax.Precision.HIGHEST
    ).astype(jnp.bfloat16)
    coupled = jnp.einsum(
        "mij,mejk->meik", coupling, combined, preferred_element_type=jnp.float32
    ).astype(jnp.bfloat16)
    partial_sum = jnp.einsum("meik,mlk->eil", coupled, coupling, preferred_element_type=jnp.float32)
    modes_all = coupling.shape[0] * lax.axis_size("mode")
    summed = summed_on_arrival(partial_sum, "mode", 1)
    return summed / modes_all


def solution(mesh):
    return jax.shard_map(
        shards,
        mesh=mesh,
        in_specs=(P("energy", "mode", None), P("mode", None, None), P("mode"), P("mode", "energy")),
        out_specs=P("energy", "mode", None),
        check_vma=False,
    )
```

profile of v0, /device:TPU:96, one launch (start us, length us, event | category | flops | bytes accessed | tf_op | source)
XLA Modules:
  0.0 263.5 jit_solution(1662050244572922762)
XLA Ops:
  6.5 0.0 copy-start
  6.5 0.0 all-gather.2.cloned.1.call-start
  6.5 0.7 all-gather.2.cloned.1.call-update
  7.3 56.1 %all-gather.2.cloned.1.call-done = f32[1,896,896]{2,1,0:T(8,128)} async-done(((f32[1,448,896]{2,1,0:T(8,128)}), f32[1,896,896]{2,1,0:T(8,128)}) %all-gather.2.cloned.1.call-update) | async-done | bytes 3211280 | tf_op jit(solution)/shard_map/all_gather | solution.py:48
  63.4 4.7 %collective-permute-start = (f32[1,896,896]{2,1,0:T(8,128)}, f32[1,896,896]{2,1,0:T(8,128)S(1)}, u32[]{:S(2)}, u32[]{:S(2)}) collective-permute-start(f32[1,896,896]{2,1,0:T(8,128)} %all-gather.2.cloned.1.call-done), channel_id=1, source_target_pairs={{0,4},{2,6},{4,8},{6,10},{8,12},{10,14},{12,16},{14,18},{16,20},{1... | collective-permute-start | bytes 9633800 | tf_op jit(solution)/shard_map/ppermute | solution.py:12
  68.0 1.9 collective-permute-start.1
  70.0 3.6 %collective-permute-start.2 = (f32[1,896,896]{2,1,0:T(8,128)}, f32[1,896,896]{2,1,0:T(8,128)S(1)}, u32[]{:S(2)}, u32[]{:S(2)}) collective-permute-start(f32[1,896,896]{2,1,0:T(8,128)} %all-gather.2.cloned.1.call-done), channel_id=1, source_target_pairs={{2,0},{4,2},{6,4},{8,6},{10,8},{12,10},{14,12},{16,14},{18,16},{20... | collective-permute-start | bytes 9633800 | tf_op jit(solution)/shard_map/ppermute | solution.py:12
  73.6 1.9 collective-permute-start.3
  76.8 61.4 %collective-permute-done = f32[1,896,896]{2,1,0:T(8,128)S(1)} collective-permute-done((f32[1,896,896]{2,1,0:T(8,128)}, f32[1,896,896]{2,1,0:T(8,128)S(1)}, u32[]{:S(2)}, u32[]{:S(2)}) %collective-permute-start) | collective-permute-done | bytes 3211296 | tf_op jit(solution)/shard_map/ppermute | solution.py:12
  138.2 0.2 constant_dynamic-update-slice_fusion.4
  138.4 0.0 copy-start.1
  138.5 32.7 %collective-permute-done.1 = f32[1,896,896]{2,1,0:T(8,128)S(1)} collective-permute-done((f32[1,896,896]{2,1,0:T(8,128)}, f32[1,896,896]{2,1,0:T(8,128)S(1)}, u32[]{:S(2)}, u32[]{:S(2)}) %collective-permute-start.1) | collective-permute-done | bytes 3211296 | tf_op jit(solution)/shard_map/ppermute | solution.py:12
  171.1 0.2 constant_dynamic-update-slice_fusion.3
  171.3 0.0 copy-done.1
  171.3 0.2 constant_dynamic-update-slice_fusion.2
  171.5 0.0 collective-permute-done.2
  171.6 0.2 constant_dynamic-update-slice_fusion.1
  171.8 8.6 %collective-permute-done.3 = f32[1,896,896]{2,1,0:T(8,128)S(1)} collective-permute-done((f32[1,896,896]{2,1,0:T(8,128)}, f32[1,896,896]{2,1,0:T(8,128)S(1)}, u32[]{:S(2)}, u32[]{:S(2)}) %collective-permute-start.3) | collective-permute-done | bytes 3211296 | tf_op jit(solution)/shard_map/ppermute | solution.py:12
  180.4 0.2 constant_dynamic-update-slice_fusion
  180.6 34.3 %fusion = bf16[1,896,896]{2,0,1:T(2,128)(2,1)S(1)} fusion(f32[5,896,896]{2,1,0:T(8,128)S(1)} %constant_dynamic-update-slice_fusion, f32[]{:T(128)} %bitcast.3, s32[]{:T(128)} %bitcast.2, f32[]{:T(128)} %bitcast.1, s32[]{:T(128)} %bitcast), kind=kOutput, calls=%fused_computation | convolution fusion | flops 48168984 | bytes 17661968 | tf_op jit(solution)/shard_map/mew,wij->meij/dot_general | solution.py:59
  214.9 0.0 copy-done
  215.0 2.0 convolution_convert_fusion
  217.0 2.0 convolution_bitcast_fusion
  219.0 34.2 %all_to_all.5 = f32[2,1,448,896]{3,2,1,0:T(8,128)} all-to-all(f32[2,1,448,896]{3,2,1,0:T(8,128)S(1)} %convolution_bitcast_fusion), channel_id=1, replica_groups=mesh['energy'=128,'mode'=2] {'mode'}, dimensions={0} | all-to-all | bytes 6422528 | tf_op jit(solution)/shard_map/all_to_all | solution.py:23
  253.2 2.3 reduce_sum.9
  255.4 1.3 multiply_bitcast_fusion
Async XLA Ops:
  6.5 208.4 %copy-start = (bf16[1,896,896]{2,1,0:T(8,128)(2,1)S(1)}, bf16[1,896,896]{2,1,0:T(8,128)(2,1)}, u32[]{:S(2)}) copy-start(bf16[1,896,896]{2,1,0:T(8,128)(2,1)} %param.5) | copy-start | bytes 4816900
  6.5 56.8 %all-gather.2.cloned.1.call-start = ((), (), s32[]{:S(2)}) async-start(), calls=%async_computation.1 | async-start | bytes 4816896 | tf_op jit(solution)/shard_map/all_gather | solution.py:48
  63.4 74.9 %collective-permute-start = (f32[1,896,896]{2,1,0:T(8,128)}, f32[1,896,896]{2,1,0:T(8,128)S(1)}, u32[]{:S(2)}, u32[]{:S(2)}) collective-permute-start(f32[1,896,896]{2,1,0:T(8,128)} %all-gather.2.cloned.1.call-done), channel_id=1, source_target_pairs={{0,4},{2,6},{4,8},{6,10},{8,12},{10,14},{12,16},{14,18},{16,20},{1... | collective-permute-start | bytes 9633800 | tf_op jit(solution)/shard_map/ppermute | solution.py:12
  68.0 103.1 %collective-permute-start.1 = (f32[1,896,896]{2,1,0:T(8,128)}, f32[1,896,896]{2,1,0:T(8,128)S(1)}, u32[]{:S(2)}, u32[]{:S(2)}) collective-permute-start(f32[1,896,896]{2,1,0:T(8,128)} %all-gather.2.cloned.1.call-done), channel_id=1, source_target_pairs={{0,2},{2,4},{4,6},{6,8},{8,10},{10,12},{12,14},{14,16},{16,18},{18... | collective-permute-start | bytes 9633800 | tf_op jit(solution)/shard_map/ppermute | solution.py:12
  70.0 101.6 %collective-permute-start.2 = (f32[1,896,896]{2,1,0:T(8,128)}, f32[1,896,896]{2,1,0:T(8,128)S(1)}, u32[]{:S(2)}, u32[]{:S(2)}) collective-permute-start(f32[1,896,896]{2,1,0:T(8,128)} %all-gather.2.cloned.1.call-done), channel_id=1, source_target_pairs={{2,0},{4,2},{6,4},{8,6},{10,8},{12,10},{14,12},{16,14},{18,16},{20... | collective-permute-start | bytes 9633800 | tf_op jit(solution)/shard_map/ppermute | solution.py:12
  73.6 106.8 %collective-permute-start.3 = (f32[1,896,896]{2,1,0:T(8,128)}, f32[1,896,896]{2,1,0:T(8,128)S(1)}, u32[]{:S(2)}, u32[]{:S(2)}) collective-permute-start(f32[1,896,896]{2,1,0:T(8,128)} %all-gather.2.cloned.1.call-done), channel_id=1, source_target_pairs={{4,0},{6,2},{8,4},{10,6},{12,8},{14,10},{16,12},{18,14},{20,16},{2... | collective-permute-start | bytes 9633800 | tf_op jit(solution)/shard_map/ppermute | solution.py:12
  138.4 32.9 %copy-start.1 = (f32[1,896,896]{2,1,0:T(8,128)S(1)}, f32[1,896,896]{2,1,0:T(8,128)}, u32[]{:S(2)}) copy-start(f32[1,896,896]{2,1,0:T(8,128)} %all-gather.2.cloned.1.call-done) | copy-start | bytes 9633796
Sparse Core Ops, SparseCore 0:
  9.2 54.1 all-gather.1
where the time goes:
time: 264 us
  waiting for transfers between devices  160 us (61%)
  matrix products  38.3 us (15%)
  blocking collectives  34.2 us (13%)
  between operations  14.8 us (6%)
  starting transfers between devices  12.1 us (5%)
  other arithmetic  3.54 us (1%)
    ppermute x4, waiting for transfers between devices, passed_along(): lax.ppermute(value, axis, [(source, source + steps) for source in range(f...  103 us
    all_gather x1, waiting for transfers between devices, shards(): full_block = lax.all_gather(spectral, 'mode', axis=1, tiled=True)  56.1 us
    dot_general x1, matrix products, shards(): jnp.einsum('mew,wij->meij', weights_table, window, precision=lax.Precisio...  34.3 us
    all_to_all x1, blocking collectives, summed_on_arrival(): lax.all_to_all(parts, axis, split_axis=0, concat_axis=0, tiled=True)  34.2 us
    ppermute x4, starting transfers between devices, passed_along(): lax.ppermute(value, axis, [(source, source + steps) for source in range(f...  12.1 us
  transfers between devices with their start and end apart: 5, of which 4 were waited for; matrix products, arithmetic and copies ran while one was open for 0% of the time, Pallas kernels for 0%

commit v1 on v0

--- a/solution.py
+++ b/solution.py
@@ -1,9 +1,20 @@
+import functools
 import jax
 import jax.numpy as jnp
 from jax import lax
 from jax.sharding import PartitionSpec as P
+from jax.lax import all_to_all, psum
 
 KMAX = 2
+
+
+def keep_up_screen_on(v0, ndim_at):
+    return jnp.concatenate(
+        all_to_all(jnp.stack(psum(1, "mode") * [v0], axis=0), "mode", 0, 0), ndim_at
+    )
+
+
+begin_the_zone = functools.partial(keep_up_screen_on, ndim_at=1)
 
 
 def passed_along(value, axis, steps):
@@ -45,7 +56,7 @@
 
 def shards(spectral, coupling, offsets, occupation):
     max_offset = KMAX
-    full_block = lax.all_gather(spectral, "mode", axis=1, tiled=True)
+    full_block = begin_the_zone(spectral)
     window = collect_rim(full_block, max_offset)
     per_device = spectral.shape[0]
     window_len = window.shape[0]

time: 264 us -> 237 us (0.90)
  waiting for transfers between devices: 160 us -> 103 us
  blocking collectives: 34.2 us -> 75 us
  between operations: 14.8 us -> 1.4 us
    all_gather x1 -> x0, waiting for transfers between devices: 56.1 us -> none  [shards(): full_block = lax.all_gather(spectral, 'mode', axis=1, tiled=True)]
    all_to_all x0 -> x1, blocking collectives: none -> 42.5 us  [keep_up_screen_on(): all_to_all(jnp.stack(psum(1, 'mode') * [v0], axis=0), 'mode', 0, 0)]
  transfers between devices with their start and end apart: 5 -> 4, of which waited for: 4 -> 3; matrix products, arithmetic and copies ran while one was open for 0% -> 0% of each run, Pallas kernels for 0% -> 0%
where the time goes in v1:
time: 237 us
  waiting for transfers between devices  103 us (43%)
  blocking collectives  75 us (32%)
  matrix products  38.3 us (16%)
  starting transfers between devices  12.5 us (5%)
  other arithmetic  5.8 us (2%)
    ppermute x4, waiting for transfers between devices, passed_along(): lax.ppermute(value, axis, [(source, source + steps) for source in range(f...  103 us
    all_to_all x1, blocking collectives, keep_up_screen_on(): all_to_all(jnp.stack(psum(1, 'mode') * [v0], axis=0), 'mode', 0, 0)  42.5 us
    dot_general x1, matrix products, shards(): jnp.einsum('mew,wij->meij', weights_table, window, precision=lax.Precisio...  34.3 us
    all_to_all x1, blocking collectives, summed_on_arrival(): lax.all_to_all(parts, axis, split_axis=0, concat_axis=0, tiled=True)  32.5 us
    ppermute x4, starting transfers between devices, passed_along(): lax.ppermute(value, axis, [(source, source + steps) for source in range(f...  12.5 us
  transfers between devices with their start and end apart: 4, of which 3 were waited for; matrix products, arithmetic and copies ran while one was open for 0% of the time, Pallas kernels for 0%

profile of v1, /device:TPU:96, one launch (start us, length us, event | category | flops | bytes accessed | tf_op | source)
XLA Modules:
  0.0 237.0 jit_solution(8332783350758990716)
XLA Ops:
  0.0 0.0 copy-start
  0.0 2.3 pad_maximum_fusion
  2.3 42.5 %all_to_all.10 = f32[2,1,448,896]{3,2,1,0:T(8,128)S(1)} all-to-all(f32[2,1,448,896]{3,2,1,0:T(8,128)S(1)} %pad_maximum_fusion), channel_id=1, replica_groups=mesh['energy'=128,'mode'=2] {'mode'}, dimensions={0} | all-to-all | bytes 6422528 | tf_op jit(solution)/shard_map/all_to_all | solution.py:13
  44.8 5.0 %collective-permute-start = (f32[1,896,896]{2,1,0:T(8,128)S(1)}, f32[1,896,896]{2,1,0:T(8,128)S(1)}, u32[]{:S(2)}, u32[]{:S(2)}) collective-permute-start(f32[1,896,896]{2,1,0:T(8,128)S(1)} %bitcast.30), channel_id=1, source_target_pairs={{0,4},{2,6},{4,8},{6,10},{8,12},{10,14},{12,16},{14,18},{16,20},{1... | collective-permute-start | bytes 9633800 | tf_op jit(solution)/shard_map/ppermute | solution.py:23
  49.8 1.9 collective-permute-start.1
  51.8 3.6 %collective-permute-start.2 = (f32[1,896,896]{2,1,0:T(8,128)S(1)}, f32[1,896,896]{2,1,0:T(8,128)S(1)}, u32[]{:S(2)}, u32[]{:S(2)}) collective-permute-start(f32[1,896,896]{2,1,0:T(8,128)S(1)} %bitcast.32), channel_id=1, source_target_pairs={{2,0},{4,2},{6,4},{8,6},{10,8},{12,10},{14,12},{16,14},{18,16},{20... | collective-permute-start | bytes 9633800 | tf_op jit(solution)/shard_map/ppermute | solution.py:23
  55.4 1.9 collective-permute-start.3
  58.6 61.1 %collective-permute-done = f32[1,896,896]{2,1,0:T(8,128)S(1)} collective-permute-done((f32[1,896,896]{2,1,0:T(8,128)S(1)}, f32[1,896,896]{2,1,0:T(8,128)S(1)}, u32[]{:S(2)}, u32[]{:S(2)}) %collective-permute-start) | collective-permute-done | bytes 3211296 | tf_op jit(solution)/shard_map/ppermute | solution.py:23
  119.8 0.2 constant_dynamic-update-slice_fusion.4
  120.0 31.2 %collective-permute-done.1 = f32[1,896,896]{2,1,0:T(8,128)S(1)} collective-permute-done((f32[1,896,896]{2,1,0:T(8,128)S(1)}, f32[1,896,896]{2,1,0:T(8,128)S(1)}, u32[]{:S(2)}, u32[]{:S(2)}) %collective-permute-start.1) | collective-permute-done | bytes 3211296 | tf_op jit(solution)/shard_map/ppermute | solution.py:23
  151.1 0.2 constant_dynamic-update-slice_fusion.3
  151.4 0.2 constant_dynamic-update-slice_fusion.2
  151.6 0.0 collective-permute-done.2
  151.6 0.2 constant_dynamic-update-slice_fusion.1
  151.8 10.6 %collective-permute-done.3 = f32[1,896,896]{2,1,0:T(8,128)S(1)} collective-permute-done((f32[1,896,896]{2,1,0:T(8,128)S(1)}, f32[1,896,896]{2,1,0:T(8,128)S(1)}, u32[]{:S(2)}, u32[]{:S(2)}) %collective-permute-start.3) | collective-permute-done | bytes 3211296 | tf_op jit(solution)/shard_map/ppermute | solution.py:23
  162.4 0.2 constant_dynamic-update-slice_fusion
  162.6 34.3 %fusion = bf16[1,896,896]{2,0,1:T(2,128)(2,1)S(1)} fusion(f32[5,896,896]{2,1,0:T(8,128)S(1)} %constant_dynamic-update-slice_fusion, f32[]{:T(128)} %bitcast.3, s32[]{:T(128)} %bitcast.2, f32[]{:T(128)} %bitcast.1, s32[]{:T(128)} %bitcast), kind=kOutput, calls=%fused_computation | convolution fusion | flops 48168984 | bytes 17661968 | tf_op jit(solution)/shard_map/mew,wij->meij/dot_general | solution.py:70
  196.9 0.0 copy-done
  196.9 2.0 convolution_convert_fusion
  198.9 2.0 convolution_bitcast_fusion
  200.9 32.5 %all_to_all.11 = f32[2,1,448,896]{3,2,1,0:T(8,128)} all-to-all(f32[2,1,448,896]{3,2,1,0:T(8,128)S(1)} %convolution_bitcast_fusion), channel_id=1, replica_groups=mesh['energy'=128,'mode'=2] {'mode'}, dimensions={0} | all-to-all | bytes 6422528 | tf_op jit(solution)/shard_map/all_to_all | solution.py:34
  233.5 2.3 reduce_sum.9
  235.7 1.3 multiply_bitcast_fusion
Async XLA Ops:
  0.0 196.9 %copy-start = (bf16[1,896,896]{2,1,0:T(8,128)(2,1)S(1)}, bf16[1,896,896]{2,1,0:T(8,128)(2,1)}, u32[]{:S(2)}) copy-start(bf16[1,896,896]{2,1,0:T(8,128)(2,1)} %param.5) | copy-start | bytes 4816900
  44.8 75.0 %collective-permute-start = (f32[1,896,896]{2,1,0:T(8,128)S(1)}, f32[1,896,896]{2,1,0:T(8,128)S(1)}, u32[]{:S(2)}, u32[]{:S(2)}) collective-permute-start(f32[1,896,896]{2,1,0:T(8,128)S(1)} %bitcast.30), channel_id=1, source_target_pairs={{0,4},{2,6},{4,8},{6,10},{8,12},{10,14},{12,16},{14,18},{16,20},{1... | collective-permute-start | bytes 9633800 | tf_op jit(solution)/shard_map/ppermute | solution.py:23
  49.8 101.3 %collective-permute-start.1 = (f32[1,896,896]{2,1,0:T(8,128)S(1)}, f32[1,896,896]{2,1,0:T(8,128)S(1)}, u32[]{:S(2)}, u32[]{:S(2)}) collective-permute-start(f32[1,896,896]{2,1,0:T(8,128)S(1)} %bitcast.31), channel_id=1, source_target_pairs={{0,2},{2,4},{4,6},{6,8},{8,10},{10,12},{12,14},{14,16},{16,18},{18... | collective-permute-start | bytes 9633800 | tf_op jit(solution)/shard_map/ppermute | solution.py:23
  51.8 99.8 %collective-permute-start.2 = (f32[1,896,896]{2,1,0:T(8,128)S(1)}, f32[1,896,896]{2,1,0:T(8,128)S(1)}, u32[]{:S(2)}, u32[]{:S(2)}) collective-permute-start(f32[1,896,896]{2,1,0:T(8,128)S(1)} %bitcast.32), channel_id=1, source_target_pairs={{2,0},{4,2},{6,4},{8,6},{10,8},{12,10},{14,12},{16,14},{18,16},{20... | collective-permute-start | bytes 9633800 | tf_op jit(solution)/shard_map/ppermute | solution.py:23
  55.4 107.0 %collective-permute-start.3 = (f32[1,896,896]{2,1,0:T(8,128)S(1)}, f32[1,896,896]{2,1,0:T(8,128)S(1)}, u32[]{:S(2)}, u32[]{:S(2)}) collective-permute-start(f32[1,896,896]{2,1,0:T(8,128)S(1)} %bitcast.33), channel_id=1, source_target_pairs={{4,0},{6,2},{8,4},{10,6},{12,8},{14,10},{16,12},{18,14},{20,16},{2... | collective-permute-start | bytes 9633800 | tf_op jit(solution)/shard_map/ppermute | solution.py:23
